TPU v7x, 256 devices: a whole 4x4x8 slice. The times are simulated.
256 devices in a mesh: ctx: 8 (over z), exp: 32 (over y, x, core).
Axes of the slice: x: 4, y: 4, z: 8, core: 2. Of those that a mesh axis runs over, the one named last changes fastest.
Arguments:
- query_rows: bfloat16 [6144, 4096], P('ctx', 'exp'), may hold values from -6 to 6
- key_rows: bfloat16 [6144, 4096], P('ctx', 'exp'), may hold values from -6 to 6
- value_rows: bfloat16 [6144, 4096], P('ctx', 'exp'), may hold values from -6 to 6
- log_decay: float32 [32, 6144], P('exp', 'ctx'), may hold values from -1 to 0
- residual: bfloat16 [6144, 3072], P(('ctx', 'exp')), may hold values from -20 to 20
- norm_gain: float32 [3072], replicated, may hold values from 0.1 to 1.9
- out_grad: bfloat16 [6144, 3072], P(('ctx', 'exp')), may hold values from -6 to 6
- experts_of: int32 [6144, 2], P(('ctx', 'exp')), may hold values from 0 to 31, all different within a row; in each aligned block of 24 rows (0 to 23, 24 to 47, ...) at most 2 rows name the same one
- route_weight: float32 [6144, 2], P(('ctx', 'exp')), may hold values from 0.1 to 0.9
- output_weight: bfloat16 [4096, 3072], P('exp'), may hold values from -0.09375 to 0.09375
- expert_gate: bfloat16 [32, 3072, 4608], P('exp', None, 'ctx'), may hold values from -0.109375 to 0.109375
- expert_up: bfloat16 [32, 3072, 4608], P('exp', None, 'ctx'), may hold values from -0.109375 to 0.109375
- expert_down: bfloat16 [32, 4608, 3072], P('exp', 'ctx'), may hold values from -0.09375 to 0.09375
Outputs:
- query_grad: bfloat16 [6144, 4096], P('ctx', 'exp')
- key_grad: bfloat16 [6144, 4096], P('ctx', 'exp')
- value_grad: bfloat16 [6144, 4096], P('ctx', 'exp')
Inputs may be any that keep to these rules, and one draw needn't show every extreme that they name: `experts_of`: in each aligned block of 24 tokens (the tokens of one device) no expert is named by more than 2 tokens, a bound that some block reaches; a token's two experts differ.
All inputs are finite; a program needn't handle non-finite values.
Results may differ from a plain program's by a relative error of at most 0.017.
Values may be sent and summed in bfloat16 or wider, within the bound.
No kernel may reach another device: no remote copies, remote signals or barrier semaphores. Data moves between devices by JAX's collectives and lax.ppermute only.
A program may use at most 128 MiB of HBM per device.

v0:
```python
import math
import jax
import jax.numpy as jnp
from jax import lax
from jax.sharding import PartitionSpec as P


def prefix(part, axis, combine, identity, reverse):
    count = lax.axis_size(axis)
    place = lax.axis_index(axis)
    ahead = count - 1 - place if reverse else place
    gathered = jax.tree.map(lambda a: lax.all_gather(a, axis), part)
    state = jax.tree.map(lambda a, e: jnp.zeros_like(a) + jnp.asarray(e, a.dtype), part, identity)

    def one(turn, state):
        source = count - 1 - turn if reverse else turn
        return combine(
            state, jax.tree.map(lambda a: lax.dynamic_index_in_dim(a, source, 0, False), gathered)
        )

    return lax.fori_loop(0, ahead, one, state)


def normalize(residual, norm_gain):
    residual_f = residual.astype(jnp.float32)
    factor = lax.rsqrt(jnp.mean(residual_f * residual_f, axis=-1, keepdims=True) + 1e-05)
    return (residual_f, factor, (residual_f * factor * norm_gain).astype(jnp.bfloat16))


def slot_table(experts_of, count, capacity):
    flat_ids = experts_of.reshape(-1)
    matches = (flat_ids[:, None] == jnp.arange(count, dtype=jnp.int32)[None, :]).astype(jnp.int32)
    before = jnp.cumsum(matches, axis=0, dtype=jnp.int32) - matches
    target = flat_ids * capacity + jnp.sum(before * matches, axis=1, dtype=jnp.int32)
    slots = jnp.arange(count * capacity, dtype=jnp.int32)
    return (slots[:, None] == target[None, :]).astype(jnp.bfloat16)


def expert_rows(row_block, gate_mat, up_mat, down_mat):
    features = gate_mat.shape[0]
    row_input = row_block[:, :features]
    row_grad = row_block[:, features:]
    gate_pre = jnp.dot(row_input, gate_mat, preferred_element_type=jnp.float32)
    up_pre = jnp.dot(row_input, up_mat, preferred_element_type=jnp.float32)
    hidden_grad = lax.dot_general(
        row_grad, down_mat, (((1,), (1,)), ((), ())), preferred_element_type=jnp.float32
    )
    gate_sig = jax.nn.sigmoid(gate_pre)
    gate_grad = (hidden_grad * up_pre * gate_sig * (1.0 + gate_pre * (1.0 - gate_sig))).astype(
        jnp.bfloat16
    )
    up_grad = (hidden_grad * gate_pre * gate_sig).astype(jnp.bfloat16)
    first = lax.dot_general(
        gate_grad, gate_mat, (((1,), (1,)), ((), ())), preferred_element_type=jnp.float32
    )
    second = lax.dot_general(
        up_grad, up_mat, (((1,), (1,)), ((), ())), preferred_element_type=jnp.float32
    )
    return first + second


def block_terms(query_part, key_part, value_part, grad_part, log_steps, score_scale):
    levels = jnp.cumsum(log_steps)
    block_total = levels[-1]
    from_start = jnp.exp(levels)
    to_end = jnp.exp(block_total - levels)
    key_state = lax.dot_general(
        key_part.astype(jnp.float32) * to_end[:, None],
        value_part.astype(jnp.float32),
        (((0,), (0,)), ((), ())),
        precision=lax.Precision.HIGHEST,
    )
    adjoint = score_scale * lax.dot_general(
        query_part.astype(jnp.float32) * from_start[:, None],
        grad_part.astype(jnp.float32),
        (((0,), (0,)), ((), ())),
        precision=lax.Precision.HIGHEST,
    )
    return (levels, jnp.exp(block_total), key_state, adjoint)


def block_grads(
    query_part, key_part, value_part, grad_part, levels, state_in, adjoint_out, score_scale
):
    block_total = levels[-1]
    from_start = jnp.exp(levels)
    to_end = jnp.exp(block_total - levels)
    token_position = jnp.arange(levels.shape[0], dtype=jnp.int32)
    causal = token_position[:, None] >= token_position[None, :]
    fading = jnp.exp(jnp.where(causal, levels[:, None] - levels[None, :], -jnp.inf))
    scores = lax.dot_general(
        query_part, key_part, (((1,), (1,)), ((), ())), preferred_element_type=jnp.float32
    )
    attn_probs = (score_scale * scores * fading).astype(jnp.bfloat16)
    grad_scores = lax.dot_general(
        grad_part, value_part, (((1,), (1,)), ((), ())), preferred_element_type=jnp.float32
    )
    pull_weights = (score_scale * grad_scores * fading).astype(jnp.bfloat16)
    grad_f = grad_part.astype(jnp.float32)
    query_out = jnp.dot(pull_weights, key_part, preferred_element_type=jnp.float32)
    query_out = query_out + score_scale * from_start[:, None] * lax.dot_general(
        grad_f, state_in, (((1,), (1,)), ((), ())), precision=lax.Precision.HIGHEST
    )
    key_out = lax.dot_general(
        pull_weights, query_part, (((0,), (0,)), ((), ())), preferred_element_type=jnp.float32
    )
    key_out = key_out + to_end[:, None] * lax.dot_general(
        value_part.astype(jnp.float32),
        adjoint_out,
        (((1,), (1,)), ((), ())),
        precision=lax.Precision.HIGHEST,
    )
    value_out = lax.dot_general(
        attn_probs, grad_part, (((0,), (0,)), ((), ())), preferred_element_type=jnp.float32
    )
    value_out = value_out + to_end[:, None] * jnp.dot(
        key_part.astype(jnp.float32), adjoint_out, precision=lax.Precision.HIGHEST
    )
    return (
        query_out.astype(jnp.bfloat16),
        key_out.astype(jnp.bfloat16),
        value_out.astype(jnp.bfloat16),
    )


def chain_link(earlier, following):
    return (earlier[0] * following[0], following[0] * earlier[1] + following[1])


def body(
    query_rows,
    key_rows,
    value_rows,
    log_decay,
    residual,
    norm_gain,
    out_grad,
    experts_of,
    route_weight,
    output_weight,
    expert_gate,
    expert_up,
    expert_down,
):
    ctx_count = lax.axis_size("ctx")
    exp_count = lax.axis_size("exp")
    token_count = residual.shape[0]
    features = residual.shape[1]
    capacity = max(2, 3 * token_count // exp_count)
    residual_f, factor, expert_input = normalize(residual, norm_gain)
    slot_onehot = slot_table(experts_of, exp_count, capacity)
    routed = (route_weight[:, :, None] * out_grad.astype(jnp.float32)[:, None, :]).astype(
        jnp.bfloat16
    )
    inputs = jnp.broadcast_to(expert_input[:, None, :], routed.shape)
    packed = jnp.concatenate([inputs, routed], axis=-1).reshape(2 * token_count, 2 * features)
    outgoing = jnp.dot(slot_onehot, packed, preferred_element_type=jnp.float32).astype(jnp.bfloat16)
    outgoing = outgoing.reshape(exp_count, capacity, 2 * features)
    gate_mat = expert_gate[0]
    up_mat = expert_up[0]
    down_mat = expert_down[0]
    arrived = lax.all_to_all(outgoing, "exp", split_axis=0, concat_axis=0, tiled=True).reshape(
        exp_count * capacity, 2 * features
    )
    partials = expert_rows(
        lax.all_gather(arrived, "ctx", axis=0, tiled=True), gate_mat, up_mat, down_mat
    )
    partials = partials.reshape(ctx_count, exp_count, capacity, features)
    summed = lax.psum_scatter(
        partials.astype(jnp.bfloat16), "ctx", scatter_dimension=0, tiled=True
    ).astype(jnp.float32)
    returned = lax.all_to_all(
        summed[0].astype(jnp.bfloat16), "exp", split_axis=0, concat_axis=0, tiled=True
    )
    per_row = lax.dot_general(
        slot_onehot,
        returned.reshape(exp_count * capacity, features),
        (((0,), (0,)), ((), ())),
        preferred_element_type=jnp.float32,
    )
    moe_grad = jnp.sum(per_row.reshape(token_count, 2, features), axis=1)
    scaled = norm_gain * moe_grad
    unit_rows = residual_f * factor
    total_grad = out_grad.astype(jnp.float32) + factor * (
        scaled - unit_rows * jnp.mean(unit_rows * scaled, axis=-1, keepdims=True)
    )
    resid_grad = total_grad.astype(jnp.bfloat16)
    attn_grad = lax.dot_general(
        lax.all_gather(resid_grad, "exp", axis=0, tiled=True),
        output_weight,
        (((1,), (1,)), ((), ())),
        preferred_element_type=jnp.float32,
    ).astype(jnp.bfloat16)
    block_len = query_rows.shape[0]
    head_size = query_rows.shape[1]
    score_scale = 1.0 / math.sqrt(head_size * block_len * ctx_count)
    levels, block_gain, key_state, adjoint = block_terms(
        query_rows, key_rows, value_rows, attn_grad, log_decay[0], score_scale
    )
    zero_state = jnp.zeros((head_size, head_size), jnp.float32)
    identity = (jnp.ones((), jnp.float32), zero_state)
    state_pair = prefix((block_gain, key_state), "ctx", chain_link, identity, False)
    adjoint_pair = prefix((block_gain, adjoint), "ctx", chain_link, identity, True)
    state_in = state_pair[1]
    adjoint_out = adjoint_pair[1]
    return block_grads(
        query_rows, key_rows, value_rows, attn_grad, levels, state_in, adjoint_out, score_scale
    )


def solution(mesh):
    placed = (
        P("ctx", "exp"),
        P("ctx", "exp"),
        P("ctx", "exp"),
        P("exp", "ctx"),
        P(("ctx", "exp"), None),
        P(),
        P(("ctx", "exp"), None),
        P(("ctx", "exp"), None),
        P(("ctx", "exp"), None),
        P("exp", None),
        P("exp", None, "ctx"),
        P("exp", None, "ctx"),
        P("exp", "ctx", None),
    )
    return jax.shard_map(
        body,
        mesh=mesh,
        in_specs=placed,
        out_specs=(P("ctx", "exp"), P("ctx", "exp"), P("ctx", "exp")),
        check_vma=False,
    )
```

profile of v0, /device:TPU:2, one launch (start us, length us, event | category | flops | bytes accessed | tf_op | source)
XLA Modules:
  0.0 386.1 jit_solution(18143667295432726540)
XLA Ops:
  8.9 1.4 reduce_window_sum.43
  14.7 1.8 concatenate.6
  16.5 1.9 mul.202
  18.4 2.3 mul.203
  23.2 2.2 convolution_convert_fusion
  25.4 2.9 reshape.141
  28.3 20.9 %all_to_all.10 = bf16[32,2,6144]{2,1,0:T(2,128)(2,1)} all-to-all(bf16[32,2,6144]{2,1,0:T(2,128)(2,1)} %reshape.141), channel_id=1, replica_groups=mesh['ctx'=8,'exp'=32] {'exp'}, dimensions={0} | all-to-all | bytes 1572864 | tf_op jit(solution)/shard_map/all_to_all | solution.py:162
  49.2 3.0 reshape.142
  52.4 74.6 %all-gather.5.cloned.1.call-done = bf16[512,6144]{1,0:T(8,128)(2,1)} async-done(((bf16[64,6144]{1,0:T(8,128)(2,1)}), bf16[512,6144]{1,0:T(8,128)(2,1)}) %all-gather.5.cloned.1.call-update) | async-done | bytes 6291472 | tf_op jit(solution)/shard_map/all_gather | solution.py:166
  127.0 6.1 %fusion.2 = f32[512,576]{0,1:T(8,128)} fusion(bf16[1,3072,576]{1,2,0:T(8,128)(2,1)} %param.27, bf16[512,6144]{1,0:T(8,128)(2,1)} %all-gather.5.cloned.1.call-done), kind=kOutput, calls=%fused_computation.6 | convolution fusion | flops 1811939328 | bytes 7864320 | tf_op jit(solution)/shard_map/dot_general | solution.py:43
  133.1 3.1 fusion.7
  136.2 11.1 %fusion = f32[512,3072]{1,0:T(8,128)} fusion(bf16[1,3072,576]{1,2,0:T(8,128)(2,1)} %param.27, f32[512,576]{0,1:T(8,128)} %fusion.7, bf16[1,3072,576]{1,2,0:T(8,128)(2,1)S(1)} %copy-done, bf16[512,6144]{1,0:T(8,128)(2,1)} %all-gather.5.cloned.1.call-done, f32[512,576]{0,1:T(8,128)} %fusion.2), kind=kOutput, calls=%fused_computation.4 | convolution fusion | flops 3626827776 | bytes 18874368 | tf_op jit(solution)/shard_map/dot_general | solution.py:53
  147.3 6.8 %add_convert_fusion = bf16[512,3072]{1,0:T(8,128)(2,1)} fusion(f32[512,3072]{1,0:T(8,128)} %fusion, bf16[1,3072,576]{1,2,0:T(8,128)(2,1)S(1)} %copy-done, f32[512,576]{0,1:T(8,128)} %fusion.7, f32[512,576]{0,1:T(8,128)} %fusion.2), kind=kOutput, calls=%fused_computation.3 | convolution fusion | flops 1816854528 | bytes 15335424 | tf_op jit(solution)/shard_map/dot_general | solution.py:56
  154.1 7.2 %convert_element_type.79 = bf16[8,32,2,3072]{3,2,1,0:T(2,128)(2,1)} reshape(bf16[512,3072]{1,0:T(8,128)(2,1)} %add_convert_fusion) | data formatting | bytes 6291456 | tf_op jit(solution)/shard_map/convert_element_type | solution.py:170
  161.3 4.4 %copy.34 = bf16[8,32,2,3072]{3,1,2,0:T(8,128)(2,1)} copy(bf16[8,32,2,3072]{3,2,1,0:T(2,128)(2,1)} %convert_element_type.79) | data formatting | bytes 6291456 | tf_op jit(solution)/shard_map/convert_element_type | solution.py:170
  165.7 45.8 %reduce-scatter.2.cloned.1.call-done = bf16[1,32,2,3072]{3,1,2,0:T(8,128)(2,1)} async-done(((bf16[8,32,2,3072]{3,1,2,0:T(8,128)(2,1)}), bf16[1,32,2,3072]{3,1,2,0:T(8,128)(2,1)}) %reduce-scatter.2.cloned.1.call-update) | async-done | bytes 393232 | tf_op jit(solution)/shard_map/reduce_scatter | solution.py:169
  211.6 2.1 copy.35
  213.7 7.3 %all-to-all-start.1 = ((bf16[32,2,3072]{2,1,0:T(2,128)(2,1)}), bf16[32,2,3072]{2,1,0:T(2,128)(2,1)}, u32[]{:S(2)}, u32[]{:S(2)}) async-start(bf16[32,2,3072]{2,1,0:T(2,128)(2,1)} %copy.35), calls=%async_computation.2 | async-start | bytes 786432 | tf_op jit(solution)/shard_map/all_to_all | solution.py:172
  221.0 1.3 iota_compare_fusion.4
  222.4 1.3 eq.47
  223.7 6.3 %all-to-all-done.1 = bf16[32,2,3072]{2,1,0:T(2,128)(2,1)} async-done(((bf16[32,2,3072]{2,1,0:T(2,128)(2,1)}), bf16[32,2,3072]{2,1,0:T(2,128)(2,1)}, u32[]{:S(2)}, u32[]{:S(2)}) %all-to-all-start.1) | async-done | bytes 393248 | tf_op jit(solution)/shard_map/all_to_all | solution.py:172
  230.0 1.9 reshape.153
  231.9 1.2 convolution_reduce_fusion
  234.3 1.8 fusion.64
  238.6 1.3 dynamic-slice
  240.6 16.3 %all-reduce = f32[8]{0:T(128)} all-reduce(f32[8]{0:T(128)S(1)} %dynamic-update-slice), channel_id=1, replica_groups=mesh['ctx'=8,'exp'=32] {'ctx'}, use_global_device_ids=true, to_apply=%add | all-reduce | flops 8 | bytes 64
  257.5 1.6 fusion.53
  259.1 27.3 %all-gather = f32[1024,128]{1,0:T(8,128)} all-gather(f32[128,128]{1,0:T(8,128)S(1)} %fusion.53), channel_id=2, replica_groups=mesh['ctx'=8,'exp'=32] {'ctx'}, dimensions={0}, use_global_device_ids=true | all-gather | bytes 589824 | tf_op jit(solution)/shard_map/all_gather | solution.py:12
  287.0 4.0 %convolution_convert_fusion.1 = bf16[768,128]{1,0:T(8,128)(2,1)S(1)} fusion(bf16[768,3072]{1,0:T(8,128)(2,1)} %all-gather.7.cloned.1.call-done, bf16[128,3072]{1,0:T(8,128)(2,1)} %param.26), kind=kOutput, calls=%fused_computation.42 | convolution fusion | flops 604078080 | bytes 5701632 | tf_op jit(solution)/shard_map/dot_general | solution.py:188
  291.7 1.5 multiply_convert_fusion.1
  293.2 3.2 fusion.22
  296.4 1.6 convolution_multiply_fusion.3
  298.1 49.7 %all-gather.1 = f32[1024,128]{1,0:T(8,128)} all-gather(f32[128,128]{1,0:T(8,128)S(1)} %convolution_multiply_fusion.3), channel_id=3, replica_groups=mesh['ctx'=8,'exp'=32] {'ctx'}, dimensions={0}, use_global_device_ids=true | all-gather | bytes 589824 | tf_op jit(solution)/shard_map/all_gather | solution.py:12
  348.4 23.6 %while.27 = (s32[]{:T(128)}, f32[128,128]{1,0:T(8,128)}, s32[]{:T(128)}, f32[8]{0:T(128)}, f32[8,128,128]{2,1,0:T(8,128)}, /*index=5*/s32[]{:T(128)}, s32[]{:T(128)}, s32[]{:T(128)}, s32[]{:T(128)}) while((s32[]{:T(128)}, f32[128,128]{1,0:T(8,128)}, s32[]{:T(128)}, f32[8]{0:T(128)}, f32[8,128,128]{2,1,0:T(8,128)}, /*index=5*/s32[]{:T(128)}, ...), condition=%wide.region_11.12_spmd, body=%wide.region_10.11_spmd.sunk | while | flops 32774 | bytes 196767 | solution.py:21
  348.4 1.2 dynamic_slice.35
  349.6 2.2 bitcast_add_fusion.5
  351.8 1.2 dynamic_slice.35
  353.0 2.2 bitcast_add_fusion.5
  356.4 2.2 bitcast_add_fusion.5
  358.5 1.2 dynamic_slice.35
  359.8 2.2 bitcast_add_fusion.5
  363.1 2.2 bitcast_add_fusion.5
  366.5 2.2 bitcast_add_fusion.5
  368.7 1.2 dynamic_slice.35
  369.9 2.2 bitcast_add_fusion.5
  372.0 1.4 fusion.34
  373.5 2.1 fusion.42
  375.6 2.5 fusion.41
  (59 shorter events, 20.3 us)
Async XLA Ops:
  7.2 129.1 %copy-start = (bf16[1,3072,576]{1,2,0:T(8,128)(2,1)S(1)}, bf16[1,3072,576]{1,2,0:T(8,128)(2,1)}, u32[]{:S(2)}) copy-start(bf16[1,3072,576]{1,2,0:T(8,128)(2,1)} %param.28) | copy-start | bytes 10616836
  7.2 119.8 %all-gather.5.cloned.1.call-start = ((), (), s32[]{:S(2)}) async-start(), calls=%async_computation.3 | async-start | bytes 7077888 | tf_op jit(solution)/shard_map/all_gather | solution.py:166
  52.2 159.4 %reduce-scatter.2.cloned.1.call-start = ((), (), s32[]{:S(2)}) async-start(), calls=%async_computation.4 | async-start | bytes 3538944 | tf_op jit(solution)/shard_map/reduce_scatter | solution.py:169
  127.0 6.1 %copy-start.8 = (bf16[512,6144]{1,0:T(8,128)(2,1)S(1)}, bf16[512,6144]{1,0:T(8,128)(2,1)}, u32[]{:S(2)}) copy-start(bf16[512,6144]{1,0:T(8,128)(2,1)} %all-gather.5.cloned.1.call-done) | copy-start | bytes 18874372
  127.0 6.1 %copy-start.9 = (bf16[1,576,3072]{2,1,0:T(8,128)(2,1)S(1)}, bf16[1,576,3072]{2,1,0:T(8,128)(2,1)}, u32[]{:S(2)}) copy-start(bf16[1,576,3072]{2,1,0:T(8,128)(2,1)} %param.29) | copy-start | bytes 10616836
  165.7 67.5 %copy-start.7 = (f32[3072]{0:T(1024)S(1)}, f32[3072]{0:T(1024)}, u32[]{:S(2)}) copy-start(f32[3072]{0:T(1024)} %param.22) | copy-start | bytes 36868
  213.7 16.3 %all-to-all-start.1 = ((bf16[32,2,3072]{2,1,0:T(2,128)(2,1)}), bf16[32,2,3072]{2,1,0:T(2,128)(2,1)}, u32[]{:S(2)}, u32[]{:S(2)}) async-start(bf16[32,2,3072]{2,1,0:T(2,128)(2,1)} %copy.35), calls=%async_computation.2 | async-start | bytes 786432 | tf_op jit(solution)/shard_map/all_to_all | solution.py:172
  221.0 66.0 %all-gather.7.cloned.1.call-start = ((), (), s32[]{:S(2)}) async-start(), calls=%async_computation.5 | async-start | bytes 4866048 | tf_op jit(solution)/shard_map/all_gather | solution.py:189
  287.0 4.7 %copy-start.4 = (bf16[768,128]{1,0:T(8,128)(2,1)S(1)}, bf16[768,128]{1,0:T(8,128)(2,1)}, u32[]{:S(2)}) copy-start(bf16[768,128]{1,0:T(8,128)(2,1)} %param.19) | copy-start | bytes 589828
  291.0 0.7 copy-start.5
  372.0 6.0 %copy-start.2 = (f32[128,128]{1,0:T(8,128)S(1)}, f32[128,128]{1,0:T(8,128)}, u32[]{:S(2)}) copy-start(f32[128,128]{1,0:T(8,128)} %get-tuple-element.131) | copy-start | bytes 196612
  372.0 6.0 %copy-start.6 = (bf16[768,128]{1,0:T(8,128)(2,1)S(1)}, bf16[768,128]{1,0:T(8,128)(2,1)}, u32[]{:S(2)}) copy-start(bf16[768,128]{1,0:T(8,128)(2,1)} %copy-done.5) | copy-start | bytes 589828
  372.0 6.4 %copy-start.1 = (bf16[768,768]{1,0:T(8,128)(2,1)S(1)}, bf16[768,768]{1,0:T(8,128)(2,1)}, u32[]{:S(2)}) copy-start(bf16[768,768]{1,0:T(8,128)(2,1)} %multiply_convert_fusion.1) | copy-start | bytes 3538948
  372.0 6.4 %copy-start.3 = (bf16[768,128]{1,0:T(8,128)(2,1)S(1)}, bf16[768,128]{1,0:T(8,128)(2,1)}, u32[]{:S(2)}) copy-start(bf16[768,128]{1,0:T(8,128)(2,1)} %param.18) | copy-start | bytes 589828
Sparse Core Ops, SparseCore 0:
  52.3 74.6 all-gather.4
  165.9 45.6 reduce-scatter.1
  236.2 48.4 all-gather.6
where the time goes:
time: 388 us; the launch traced here: 386 us
  waiting for transfers between devices  127 us (33%)
  blocking collectives  114 us (29%)
  matrix products  50 us (13%)
  local copies, waits for them, and re-layouts  45.2 us (12%)
  other arithmetic  27.8 us (7%)
  between operations  14.5 us (4%)
  starting transfers between devices  7.6 us (2%)
    all_gather x2, blocking collectives, prefix(): gathered = jax.tree.map(lambda a: lax.all_gather(a, axis), part)  77 us
    all_gather x1, waiting for transfers between devices, body(): lax.all_gather(arrived, 'ctx', axis=0, tiled=True)  74.6 us
    reduce_scatter x1, waiting for transfers between devices, body(): lax.psum_scatter(partials.astype(jnp.bfloat16), 'ctx', scatter_dimension=...  45.8 us
    all_to_all x1, blocking collectives, body(): lax.all_to_all(outgoing, 'exp', split_axis=0, concat_axis=0, tiled=True)  20.9 us
    unnamed x1, blocking collectives  16.3 us
    add x7, other arithmetic, chain_link(): return (earlier[0] * following[0], following[0] * earlier[1] + following[1])  15.1 us
    convert_element_type x2, local copies, waits for them, and re-layouts, body(): partials.astype(jnp.bfloat16)  11.6 us
    dot_general x1, matrix products, expert_rows(): lax.dot_general(gate_grad, gate_mat, (((1,), (1,)), ((), ())), preferred_...  11.1 us
  transfers between devices with their start and end apart: 4, of which 3 were waited for; matrix products, arithmetic and copies ran while one was open for 2% of the time, Pallas kernels for 0%

commit v1 on v0

--- a/solution.py
+++ b/solution.py
@@ -163,7 +163,12 @@
         exp_count * capacity, 2 * features
     )
     partials = expert_rows(
-        lax.all_gather(arrived, "ctx", axis=0, tiled=True), gate_mat, up_mat, down_mat
+        jnp.concatenate(
+            lax.all_to_all(jnp.stack([arrived] * lax.axis_size("ctx")), "ctx", 0, 0), axis=0
+        ),
+        gate_mat,
+        up_mat,
+        down_mat,
     )
     partials = partials.reshape(ctx_count, exp_count, capacity, features)
     summed = lax.psum_scatter(

time: 388 us -> 459 us (1.18)
  blocking collectives: 114 us -> 264 us
  waiting for transfers between devices: 127 us -> 47.2 us
    all_to_all x0 -> x1, blocking collectives: none -> 150 us  [body(): lax.all_to_all(jnp.stack([arrived] * lax.axis_size('ctx')), 'ctx', 0, 0)]
    all_gather x1 -> x0, waiting for transfers between devices: 74.6 us -> none  [body(): lax.all_gather(arrived, 'ctx', axis=0, tiled=True)]
    reduce_scatter x1, waiting for transfers between devices: 45.8 us -> 40.9 us  [body(): lax.psum_scatter(partials.astype(jnp.bfloat16), 'ctx', scatter_dimension=...]
    another operation x1 -> x3, local copies, waits for them, and re-layouts: 0.12 us -> 4.97 us  [the longest x2 4.85 us: body(): jnp.stack([arrived] * lax.axis_size('ctx'))]
  transfers between devices with their start and end apart: 4 -> 3, of which waited for: 3 -> 2; matrix products, arithmetic and copies ran while one was open for 2% -> 2% of each run, Pallas kernels for 0% -> 0%
where the time goes in v1:
time: 459 us; the launch traced here: 457 us
  blocking collectives  264 us (58%)
  local copies, waits for them, and re-layouts  48.7 us (11%)
  waiting for transfers between devices  47.2 us (10%)
  matrix products  47 us (10%)
  other arithmetic  27.7 us (6%)
  between operations  14.8 us (3%)
  starting transfers between devices  7.51 us (2%)
    all_to_all x1, blocking collectives, body(): lax.all_to_all(jnp.stack([arrived] * lax.axis_size('ctx')), 'ctx', 0, 0)  150 us
    all_gather x2, blocking collectives, prefix(): gathered = jax.tree.map(lambda a: lax.all_gather(a, axis), part)  77.1 us
    reduce_scatter x1, waiting for transfers between devices, body(): lax.psum_scatter(partials.astype(jnp.bfloat16), 'ctx', scatter_dimension=...  40.9 us
    all_to_all x1, blocking collectives, body(): lax.all_to_all(outgoing, 'exp', split_axis=0, concat_axis=0, tiled=True)  20.9 us
    unnamed x1, blocking collectives  16.1 us
    add x7, other arithmetic, chain_link(): return (earlier[0] * following[0], following[0] * earlier[1] + following[1])  15.1 us
    convert_element_type x2, local copies, waits for them, and re-layouts, body(): partials.astype(jnp.bfloat16)  11.7 us
    dot_general x1, matrix products, expert_rows(): lax.dot_general(gate_grad, gate_mat, (((1,), (1,)), ((), ())), preferred_...  11.1 us
  transfers between devices with their start and end apart: 3, of which 2 were waited for; matrix products, arithmetic and copies ran while one was open for 2% of the time, Pallas kernels for 0%

profile of v1, /device:TPU:2, one launch (start us, length us, event | category | flops | bytes accessed | tf_op | source)
XLA Modules:
  0.0 457.3 jit_solution(12713695408041742184)
XLA Ops:
  8.9 1.4 reduce_window_sum.43
  14.7 1.8 concatenate.6
  16.5 1.9 mul.202
  18.4 2.3 mul.203
  23.2 2.2 convolution_convert_fusion
  25.4 2.9 reshape.143
  28.3 20.9 %all_to_all.15 = bf16[32,2,6144]{2,1,0:T(2,128)(2,1)} all-to-all(bf16[32,2,6144]{2,1,0:T(2,128)(2,1)} %reshape.143), channel_id=1, replica_groups=mesh['ctx'=8,'exp'=32] {'exp'}, dimensions={0} | all-to-all | bytes 1572864 | tf_op jit(solution)/shard_map/all_to_all | solution.py:162
  49.2 3.0 stack_reshape.2
  52.1 1.9 stack.3
  54.0 150.1 %all_to_all.16 = bf16[8,64,6144]{2,1,0:T(8,128)(2,1)S(1)} all-to-all(bf16[8,64,6144]{2,1,0:T(8,128)(2,1)S(1)} %stack.3), channel_id=1, replica_groups=mesh['ctx'=8,'exp'=32] {'ctx'}, dimensions={0} | all-to-all | bytes 12582912 | tf_op jit(solution)/shard_map/all_to_all | solution.py:167
  204.2 3.0 fusion.2
  208.8 3.1 fusion.7
  211.9 11.1 %fusion = f32[512,3072]{1,0:T(8,128)} fusion(bf16[1,3072,576]{1,2,0:T(8,128)(2,1)} %param.27, f32[512,576]{0,1:T(8,128)} %fusion.7, bf16[1,3072,576]{1,2,0:T(8,128)(2,1)S(1)} %copy-done, bf16[512,6144]{1,0:T(8,128)(2,1)} %bitcast.78, f32[512,576]{0,1:T(8,128)} %fusion.2), kind=kOutput, calls=%fused_computation.4 | convolution fusion | flops 3626827776 | bytes 18874368 | tf_op jit(solution)/shard_map/dot_general | solution.py:53
  223.0 6.9 %add_convert_fusion = bf16[512,3072]{1,0:T(8,128)(2,1)} fusion(f32[512,3072]{1,0:T(8,128)} %fusion, bf16[1,3072,576]{1,2,0:T(8,128)(2,1)S(1)} %copy-done, f32[512,576]{0,1:T(8,128)} %fusion.7, f32[512,576]{0,1:T(8,128)} %fusion.2), kind=kOutput, calls=%fused_computation.3 | convolution fusion | flops 1816854528 | bytes 15335424 | tf_op jit(solution)/shard_map/dot_general | solution.py:56
  229.8 7.2 %convert_element_type.79 = bf16[8,32,2,3072]{3,2,1,0:T(2,128)(2,1)} reshape(bf16[512,3072]{1,0:T(8,128)(2,1)} %add_convert_fusion) | data formatting | bytes 6291456 | tf_op jit(solution)/shard_map/convert_element_type | solution.py:175
  237.1 4.4 copy.34
  241.5 40.9 %reduce-scatter.2.cloned.1.call-done = bf16[1,32,2,3072]{3,1,2,0:T(8,128)(2,1)} async-done(((bf16[8,32,2,3072]{3,1,2,0:T(8,128)(2,1)}), bf16[1,32,2,3072]{3,1,2,0:T(8,128)(2,1)}) %reduce-scatter.2.cloned.1.call-update) | async-done | bytes 393232 | tf_op jit(solution)/shard_map/reduce_scatter | solution.py:174
  282.4 2.1 copy.35
  284.5 7.4 %all-to-all-start.2 = ((bf16[32,2,3072]{2,1,0:T(2,128)(2,1)}), bf16[32,2,3072]{2,1,0:T(2,128)(2,1)}, u32[]{:S(2)}, u32[]{:S(2)}) async-start(bf16[32,2,3072]{2,1,0:T(2,128)(2,1)} %copy.35), calls=%async_computation.3 | async-start | bytes 786432 | tf_op jit(solution)/shard_map/all_to_all | solution.py:177
  292.0 1.3 iota_compare_fusion.4
  293.3 1.3 eq.47
  294.6 6.3 %all-to-all-done.2 = bf16[32,2,3072]{2,1,0:T(2,128)(2,1)} async-done(((bf16[32,2,3072]{2,1,0:T(2,128)(2,1)}), bf16[32,2,3072]{2,1,0:T(2,128)(2,1)}, u32[]{:S(2)}, u32[]{:S(2)}) %all-to-all-start.2) | async-done | bytes 393248 | tf_op jit(solution)/shard_map/all_to_all | solution.py:177
  301.0 1.9 reshape.155
  302.9 1.2 convolution_reduce_fusion
  305.3 1.8 fusion.64
  309.5 1.3 dynamic-slice
  311.6 16.1 %all-reduce = f32[8]{0:T(128)} all-reduce(f32[8]{0:T(128)S(1)} %dynamic-update-slice), channel_id=1, replica_groups=mesh['ctx'=8,'exp'=32] {'ctx'}, use_global_device_ids=true, to_apply=%add | all-reduce | flops 8 | bytes 64
  328.2 1.6 fusion.53
  329.9 27.3 %all-gather = f32[1024,128]{1,0:T(8,128)} all-gather(f32[128,128]{1,0:T(8,128)S(1)} %fusion.53), channel_id=2, replica_groups=mesh['ctx'=8,'exp'=32] {'ctx'}, dimensions={0}, use_global_device_ids=true | all-gather | bytes 589824 | tf_op jit(solution)/shard_map/all_gather | solution.py:12
  357.8 4.0 convolution_convert_fusion.1
  362.5 1.5 multiply_convert_fusion.1
  364.0 3.2 fusion.22
  367.2 1.6 convolution_multiply_fusion.3
  368.9 49.8 %all-gather.1 = f32[1024,128]{1,0:T(8,128)} all-gather(f32[128,128]{1,0:T(8,128)S(1)} %convolution_multiply_fusion.3), channel_id=3, replica_groups=mesh['ctx'=8,'exp'=32] {'ctx'}, dimensions={0}, use_global_device_ids=true | all-gather | bytes 589824 | tf_op jit(solution)/shard_map/all_gather | solution.py:12
  419.3 23.6 %while.27 = (s32[]{:T(128)}, f32[128,128]{1,0:T(8,128)}, s32[]{:T(128)}, f32[8]{0:T(128)}, f32[8,128,128]{2,1,0:T(8,128)}, /*index=5*/s32[]{:T(128)}, s32[]{:T(128)}, s32[]{:T(128)}, s32[]{:T(128)}) while((s32[]{:T(128)}, f32[128,128]{1,0:T(8,128)}, s32[]{:T(128)}, f32[8]{0:T(128)}, f32[8,128,128]{2,1,0:T(8,128)}, /*index=5*/s32[]{:T(128)}, ...), condition=%wide.region_11.12_spmd, body=%wide.region_10.11_spmd.sunk | while | flops 32774 | bytes 196767 | solution.py:21
  419.3 1.2 dynamic_slice.35
  420.5 2.2 bitcast_add_fusion.5
  422.6 1.2 dynamic_slice.35
  423.9 2.2 bitcast_add_fusion.5
  427.2 2.2 bitcast_add_fusion.5
  430.6 2.2 bitcast_add_fusion.5
  432.8 1.2 dynamic_slice.35
  434.0 2.2 bitcast_add_fusion.5
  437.3 2.2 bitcast_add_fusion.5
  440.7 2.2 bitcast_add_fusion.5
  442.9 1.4 fusion.34
  444.3 2.1 fusion.42
  446.4 2.5 fusion.41
  (60 shorter events, 22.9 us)
Async XLA Ops:
  7.2 204.7 %copy-start = (bf16[1,3072,576]{1,2,0:T(8,128)(2,1)S(1)}, bf16[1,3072,576]{1,2,0:T(8,128)(2,1)}, u32[]{:S(2)}) copy-start(bf16[1,3072,576]{1,2,0:T(8,128)(2,1)} %param.28) | copy-start | bytes 10616836
  7.2 275.2 %reduce-scatter.2.cloned.1.call-start = ((), (), s32[]{:S(2)}) async-start(), calls=%async_computation.4 | async-start | bytes 3538944 | tf_op jit(solution)/shard_map/reduce_scatter | solution.py:174
  54.0 150.2 %copy-start.10 = (bf16[1,3072,576]{1,2,0:T(8,128)(2,1)S(1)}, bf16[1,3072,576]{1,2,0:T(8,128)(2,1)}, u32[]{:S(2)}) copy-start(bf16[1,3072,576]{1,2,0:T(8,128)(2,1)} %param.27) | copy-start | bytes 10616836
  204.2 3.7 copy-start.1
  204.2 4.6 %copy-start.9 = (bf16[1,576,3072]{2,1,0:T(8,128)(2,1)S(1)}, bf16[1,576,3072]{2,1,0:T(8,128)(2,1)}, u32[]{:S(2)}) copy-start(bf16[1,576,3072]{2,1,0:T(8,128)(2,1)} %param.29) | copy-start | bytes 10616836
  241.5 62.7 %copy-start.8 = (f32[3072]{0:T(1024)S(1)}, f32[3072]{0:T(1024)}, u32[]{:S(2)}) copy-start(f32[3072]{0:T(1024)} %param.22) | copy-start | bytes 36868
  284.5 16.5 %all-to-all-start.2 = ((bf16[32,2,3072]{2,1,0:T(2,128)(2,1)}), bf16[32,2,3072]{2,1,0:T(2,128)(2,1)}, u32[]{:S(2)}, u32[]{:S(2)}) async-start(bf16[32,2,3072]{2,1,0:T(2,128)(2,1)} %copy.35), calls=%async_computation.3 | async-start | bytes 786432 | tf_op jit(solution)/shard_map/all_to_all | solution.py:177
  292.0 65.9 %all-gather.4.cloned.1.call-start = ((), (), s32[]{:S(2)}) async-start(), calls=%async_computation.5 | async-start | bytes 4866048 | tf_op jit(solution)/shard_map/all_gather | solution.py:194
  357.8 4.7 %copy-start.5 = (bf16[768,128]{1,0:T(8,128)(2,1)S(1)}, bf16[768,128]{1,0:T(8,128)(2,1)}, u32[]{:S(2)}) copy-start(bf16[768,128]{1,0:T(8,128)(2,1)} %param.19) | copy-start | bytes 589828
  361.8 0.7 copy-start.6
  442.9 6.0 %copy-start.3 = (f32[128,128]{1,0:T(8,128)S(1)}, f32[128,128]{1,0:T(8,128)}, u32[]{:S(2)}) copy-start(f32[128,128]{1,0:T(8,128)} %get-tuple-element.131) | copy-start | bytes 196612
  442.9 6.0 %copy-start.7 = (bf16[768,128]{1,0:T(8,128)(2,1)S(1)}, bf16[768,128]{1,0:T(8,128)(2,1)}, u32[]{:S(2)}) copy-start(bf16[768,128]{1,0:T(8,128)(2,1)} %copy-done.6) | copy-start | bytes 589828
  442.9 6.4 %copy-start.2 = (bf16[768,768]{1,0:T(8,128)(2,1)S(1)}, bf16[768,768]{1,0:T(8,128)(2,1)}, u32[]{:S(2)}) copy-start(bf16[768,768]{1,0:T(8,128)(2,1)} %multiply_convert_fusion.1) | copy-start | bytes 3538948
  442.9 6.4 %copy-start.4 = (bf16[768,128]{1,0:T(8,128)(2,1)S(1)}, bf16[768,128]{1,0:T(8,128)(2,1)}, u32[]{:S(2)}) copy-start(bf16[768,128]{1,0:T(8,128)(2,1)} %param.18) | copy-start | bytes 589828
Sparse Core Ops, SparseCore 0:
  241.6 40.6 reduce-scatter.1
  307.2 48.2 all-gather.3
